TPU v7x, 32 devices: a whole 2x2x4 slice. The times are simulated.
32 devices in a mesh: fsdp: 8 (over z, x), replica: 4 (over y, core).
Axes of the slice: x: 2, y: 2, z: 4, core: 2. Of those that a mesh axis runs over, the one named last changes fastest.
Arguments:
- layer_input: bfloat16 [32, 1024, 768], P(('fsdp', 'replica')), may hold values from -6 to 6
- cotangent: bfloat16 [32, 1024, 768], P(('fsdp', 'replica')), may hold values from -6 to 6
- segment_ids: int32 [32, 1024], P(('fsdp', 'replica')), may hold values from 0 to 4, as said below
- pad_mask: int32 [32, 1024], P(('fsdp', 'replica')), may hold values from 0 to 1, as said below
- ln1_gain: bfloat16 [768], P('fsdp'), may hold values from 0.5 to 1.5
- ln1_bias: bfloat16 [768], P('fsdp'), may hold values from -1.1953125 to 1.1953125
- w_qkv: bfloat16 [768, 2304], P('fsdp'), may hold values from -0.21875 to 0.21875
- b_qkv: bfloat16 [2304], P('fsdp'), may hold values from -1.1953125 to 1.1953125
- w_out: bfloat16 [768, 768], P('fsdp'), may hold values from -1.25 to 1.25
- b_out: bfloat16 [768], P('fsdp'), may hold values from -1.1953125 to 1.1953125
- ln2_gain: bfloat16 [768], P('fsdp'), may hold values from 0.5 to 1.5
- ln2_bias: bfloat16 [768], P('fsdp'), may hold values from -1.1953125 to 1.1953125
- w_up: bfloat16 [768, 3072], P('fsdp'), may hold values from -0.21875 to 0.21875
- b_up: bfloat16 [3072], P('fsdp'), may hold values from -1.1953125 to 1.1953125
- w_down: bfloat16 [3072, 768], P('fsdp'), may hold values from -0.109375 to 0.109375
- b_down: bfloat16 [768], P('fsdp'), may hold values from -1.1953125 to 1.1953125
Outputs:
- layer_out: bfloat16 [32, 1024, 768], P(('fsdp', 'replica'))
- input_grad: bfloat16 [32, 1024, 768], P(('fsdp', 'replica'))
- grad_ln1_gain: float32 [768], P('fsdp')
- grad_ln1_bias: float32 [768], P('fsdp')
- grad_w_qkv: float32 [768, 2304], P('fsdp')
- grad_b_qkv: float32 [2304], P('fsdp')
- grad_w_out: float32 [768, 768], P('fsdp')
- grad_b_out: float32 [768], P('fsdp')
- grad_ln2_gain: float32 [768], P('fsdp')
- grad_ln2_bias: float32 [768], P('fsdp')
- grad_w_up: float32 [768, 3072], P('fsdp')
- grad_b_up: float32 [3072], P('fsdp')
- grad_w_down: float32 [3072, 768], P('fsdp')
- grad_b_down: float32 [768], P('fsdp')
Inputs may be any that keep to these rules, and one draw needn't show every extreme that they name: `segment_ids`: each row packs 4 genes numbered 0 to 3 in order from its start, each of 128 to 256 codons, never falling along a row, and 4 on the padded tail; in every row one gene has exactly 256 codons and another exactly 128. `pad_mask`: 1 exactly where segment_ids is under 4; every row ends in at least 128 padded codons.
All inputs are finite; a program needn't handle non-finite values.
Results may differ from a plain program's by a relative error of at most 0.014.
Values may be sent and summed in bfloat16 or wider, within the bound.
No kernel may reach another device: no remote copies, remote signals or barrier semaphores. Data moves between devices by JAX's collectives and lax.ppermute only.
A program may use at most 320 MiB of HBM per device.

v0:
```python
import math
import jax
import jax.numpy as jnp
from jax import lax
from jax.sharding import PartitionSpec as P

HEADS = 12
HEAD_DIM = 64
GENES = 4
EPSILON = 1e-05
NEG_FILL = -1000000000.0


def contract_rows(left_matrix, right_matrix):
    return lax.dot_general(
        left_matrix, right_matrix, (((0,), (0,)), ((), ())), preferred_element_type=jnp.float32
    )


def times_transpose(left_matrix, right_matrix):
    return lax.dot_general(
        left_matrix, right_matrix, (((1,), (1,)), ((), ())), preferred_element_type=jnp.float32
    )


def layer_norm(inputs, gain_vector, bias_vector):
    centered = inputs - jnp.mean(inputs, -1, keepdims=True)
    variance = jnp.mean(centered * centered, -1, keepdims=True)
    return centered * lax.rsqrt(variance + EPSILON) * gain_vector + bias_vector


def rotate(tensor, cosine_table, sine_table):
    half_dim = tensor.shape[-1] // 2
    first_half = tensor[..., :half_dim]
    second_half = tensor[..., half_dim:]
    return jnp.concatenate(
        [
            first_half * cosine_table - second_half * sine_table,
            second_half * cosine_table + first_half * sine_table,
        ],
        -1,
    )


def exact_gelu(inputs):
    return jax.nn.gelu(inputs, approximate=False)


def rotary_tables(positions):
    frequency = jnp.power(10000.0, jnp.arange(HEAD_DIM // 2, dtype=jnp.float32) * (-2.0 / HEAD_DIM))
    angles = positions.astype(jnp.float32)[..., None] * frequency
    return (jnp.cos(angles)[..., None, :], jnp.sin(angles)[..., None, :])


def gene_positions(segments):
    slot_ids = jnp.arange(GENES + 1, dtype=jnp.int32)
    slot_hits = segments[..., :, None] == slot_ids
    counts = jnp.sum(slot_hits.astype(jnp.int32), -2)
    starts = jnp.cumsum(counts, -1) - counts
    gene_start = jnp.sum(jnp.where(slot_hits, starts[..., None, :], 0), -1)
    return jnp.arange(segments.shape[-1], dtype=jnp.int32) - gene_start


def pair_mask(block_segments, block_valid, block_start, segments, valid_codons):
    row_ids = block_start + jnp.arange(block_segments.shape[0], dtype=jnp.int32)
    column_ids = jnp.arange(segments.shape[0], dtype=jnp.int32)
    same_gene = (
        (block_segments[:, None] == segments[None, :])
        & (block_valid[:, None] > 0)
        & (valid_codons[None, :] > 0)
    )
    return same_gene | (row_ids[:, None] == column_ids[None, :])


def block_scores(
    block_queries, key_rows, block_segments, block_valid, block_start, segments, valid_codons
):
    scores = jnp.einsum(
        "qhd,khd->hqk", block_queries, key_rows, preferred_element_type=jnp.float32
    ) * (1.0 / math.sqrt(HEAD_DIM))
    allowed = pair_mask(block_segments, block_valid, block_start, segments, valid_codons)
    return jnp.where(allowed[None], scores, NEG_FILL)


def split_blocks(queries, segments, valid_codons, block_rows):
    block_count = queries.shape[0] // block_rows
    starts = jnp.arange(block_count, dtype=jnp.int32) * block_rows
    return (
        queries.reshape(block_count, block_rows, HEADS, HEAD_DIM),
        segments.reshape(block_count, block_rows),
        valid_codons.reshape(block_count, block_rows),
        starts,
    )


def attend_forward(queries, key_rows, value_rows, segments, valid_codons, block_rows):
    length = queries.shape[0]

    def one_block(running, block_item):
        block_queries, block_segments, block_valid, block_start = block_item
        scores = block_scores(
            block_queries,
            key_rows,
            block_segments,
            block_valid,
            block_start,
            segments,
            valid_codons,
        )
        row_peak = jnp.max(scores, -1, keepdims=True)
        shifted = jnp.exp(scores - row_peak)
        row_total = jnp.sum(shifted, -1, keepdims=True)
        weights = (shifted / row_total).astype(jnp.bfloat16)
        attended = jnp.einsum(
            "hqk,khd->qhd", weights, value_rows, preferred_element_type=jnp.float32
        )
        log_total = (row_peak + jnp.log(row_total))[..., 0]
        return (running, (attended, log_total))

    ignored, (attended, log_total) = lax.scan(
        one_block,
        jnp.zeros((), jnp.float32),
        split_blocks(queries, segments, valid_codons, block_rows),
    )
    return (attended.reshape(length, HEADS, HEAD_DIM), log_total)


def attend_backward(
    queries, key_rows, value_rows, attended_grad, log_total, segments, valid_codons, block_rows
):
    length = queries.shape[0]
    block_queries_all, block_segments_all, block_valid_all, starts = split_blocks(
        queries, segments, valid_codons, block_rows
    )
    grad_blocks = attended_grad.reshape(block_queries_all.shape)
    score_scale = 1.0 / math.sqrt(HEAD_DIM)

    def one_block(running, block_item):
        key_grad, value_grad = running
        block_queries, block_grad, block_log, block_segments, block_valid, block_start = block_item
        scores = block_scores(
            block_queries,
            key_rows,
            block_segments,
            block_valid,
            block_start,
            segments,
            valid_codons,
        )
        weights = jnp.exp(scores - block_log[..., None])
        weight_grad = jnp.einsum(
            "qhd,khd->hqk", block_grad, value_rows, preferred_element_type=jnp.float32
        )
        row_dot = jnp.sum(weights * weight_grad, -1, keepdims=True)
        score_grad = (weights * (weight_grad - row_dot)).astype(jnp.bfloat16)
        query_grad = (
            jnp.einsum("hqk,khd->qhd", score_grad, key_rows, preferred_element_type=jnp.float32)
            * score_scale
        )
        key_grad = (
            key_grad
            + jnp.einsum(
                "hqk,qhd->khd", score_grad, block_queries, preferred_element_type=jnp.float32
            )
            * score_scale
        )
        value_grad = value_grad + jnp.einsum(
            "hqk,qhd->khd",
            weights.astype(jnp.bfloat16),
            block_grad,
            preferred_element_type=jnp.float32,
        )
        return ((key_grad, value_grad), query_grad)

    zero_grad = jnp.zeros(key_rows.shape, jnp.float32)
    scanned = (
        block_queries_all,
        grad_blocks,
        log_total,
        block_segments_all,
        block_valid_all,
        starts,
    )
    (key_grad, value_grad), query_grad = lax.scan(one_block, (zero_grad, zero_grad), scanned)
    return (query_grad.reshape(length, HEADS, HEAD_DIM), key_grad, value_grad)


def body(
    layer_input,
    cotangent,
    segment_ids,
    pad_mask,
    ln1_gain,
    ln1_bias,
    w_qkv,
    b_qkv,
    w_out,
    b_out,
    ln2_gain,
    ln2_bias,
    w_up,
    b_up,
    w_down,
    b_down,
):
    gain_one, bias_one, qkv_weight, qkv_bias, out_weight, out_bias = (
        lax.all_gather(ln1_gain, "fsdp", axis=0, tiled=True),
        lax.all_gather(ln1_bias, "fsdp", axis=0, tiled=True),
        lax.all_gather(w_qkv, "fsdp", axis=0, tiled=True),
        lax.all_gather(b_qkv, "fsdp", axis=0, tiled=True),
        lax.all_gather(w_out, "fsdp", axis=0, tiled=True),
        lax.all_gather(b_out, "fsdp", axis=0, tiled=True),
    )
    gain_two, bias_two, up_weight, up_bias, down_weight, down_bias = (
        lax.all_gather(ln2_gain, "fsdp", axis=0, tiled=True),
        lax.all_gather(ln2_bias, "fsdp", axis=0, tiled=True),
        lax.all_gather(w_up, "fsdp", axis=0, tiled=True),
        lax.all_gather(b_up, "fsdp", axis=0, tiled=True),
        lax.all_gather(w_down, "fsdp", axis=0, tiled=True),
        lax.all_gather(b_down, "fsdp", axis=0, tiled=True),
    )
    length = layer_input.shape[1]
    model_width = layer_input.shape[2]
    block_rows = min(512, length)
    segments = segment_ids[0]
    valid_codons = pad_mask[0]
    cosine_table, sine_table = rotary_tables(gene_positions(segments))
    inputs = layer_input[0].astype(jnp.float32)
    normed, norm_one_back = jax.vjp(
        layer_norm, inputs, gain_one.astype(jnp.float32), bias_one.astype(jnp.float32)
    )
    normed = normed.astype(jnp.bfloat16)
    projected = jnp.dot(normed, qkv_weight, preferred_element_type=jnp.float32) + qkv_bias.astype(
        jnp.float32
    )
    head_shape = (length, HEADS, HEAD_DIM)
    queries = rotate(
        projected[:, :model_width].reshape(head_shape), cosine_table, sine_table
    ).astype(jnp.bfloat16)
    key_rows = rotate(
        projected[:, model_width : 2 * model_width].reshape(head_shape), cosine_table, sine_table
    ).astype(jnp.bfloat16)
    value_rows = projected[:, 2 * model_width :].reshape(head_shape).astype(jnp.bfloat16)
    attended, log_total = attend_forward(
        queries, key_rows, value_rows, segments, valid_codons, block_rows
    )
    attended = attended.reshape(length, model_width).astype(jnp.bfloat16)
    middle = (
        inputs
        + jnp.dot(attended, out_weight, preferred_element_type=jnp.float32)
        + out_bias.astype(jnp.float32)
    )
    normed_two, norm_two_back = jax.vjp(
        layer_norm, middle, gain_two.astype(jnp.float32), bias_two.astype(jnp.float32)
    )
    normed_two = normed_two.astype(jnp.bfloat16)
    hidden = jnp.dot(normed_two, up_weight, preferred_element_type=jnp.float32) + up_bias.astype(
        jnp.float32
    )
    activated, gelu_back = jax.vjp(exact_gelu, hidden)
    activated = activated.astype(jnp.bfloat16)
    layer_out = (
        middle
        + jnp.dot(activated, down_weight, preferred_element_type=jnp.float32)
        + down_bias.astype(jnp.float32)
    ).astype(jnp.bfloat16)
    up_weight_back, down_weight_back = (
        lax.all_gather(w_up, "fsdp", axis=0, tiled=True),
        lax.all_gather(w_down, "fsdp", axis=0, tiled=True),
    )
    out_grad_rows = cotangent[0]
    grad_down_bias = jnp.sum(out_grad_rows.astype(jnp.float32), 0)
    (hidden_grad,) = gelu_back(times_transpose(out_grad_rows, down_weight_back))
    hidden_grad = hidden_grad.astype(jnp.bfloat16)
    grad_up_bias = jnp.sum(hidden_grad.astype(jnp.float32), 0)
    middle_grad, grad_gain_two, grad_bias_two = norm_two_back(
        times_transpose(hidden_grad, up_weight_back)
    )
    middle_grad = middle_grad + out_grad_rows.astype(jnp.float32)
    grad_up_weight = contract_rows(normed_two, hidden_grad)
    grad_down_weight = contract_rows(activated, out_grad_rows)
    ffn_sums = (
        lax.psum_scatter(grad_gain_two, "fsdp", scatter_dimension=0, tiled=True),
        lax.psum_scatter(grad_bias_two, "fsdp", scatter_dimension=0, tiled=True),
        lax.psum_scatter(grad_up_weight, "fsdp", scatter_dimension=0, tiled=True),
        lax.psum_scatter(grad_up_bias, "fsdp", scatter_dimension=0, tiled=True),
        lax.psum_scatter(grad_down_weight, "fsdp", scatter_dimension=0, tiled=True),
        lax.psum_scatter(grad_down_bias, "fsdp", scatter_dimension=0, tiled=True),
    )
    qkv_weight_back, out_weight_back = (
        lax.all_gather(w_qkv, "fsdp", axis=0, tiled=True),
        lax.all_gather(w_out, "fsdp", axis=0, tiled=True),
    )
    branch_grad = middle_grad.astype(jnp.bfloat16)
    grad_out_bias = jnp.sum(branch_grad.astype(jnp.float32), 0)
    attended_grad = (
        times_transpose(branch_grad, out_weight_back).astype(jnp.bfloat16).reshape(head_shape)
    )
    query_grad, key_grad, value_grad = attend_backward(
        queries, key_rows, value_rows, attended_grad, log_total, segments, valid_codons, block_rows
    )
    projected_grad = jnp.concatenate(
        [
            rotate(query_grad, cosine_table, -sine_table).reshape(length, model_width),
            rotate(key_grad, cosine_table, -sine_table).reshape(length, model_width),
            value_grad.reshape(length, model_width),
        ],
        1,
    ).astype(jnp.bfloat16)
    grad_qkv_bias = jnp.sum(projected_grad.astype(jnp.float32), 0)
    input_part, grad_gain_one, grad_bias_one = norm_one_back(
        times_transpose(projected_grad, qkv_weight_back)
    )
    input_grad = (middle_grad + input_part).astype(jnp.bfloat16)
    grad_out_weight = contract_rows(attended, branch_grad)
    grad_qkv_weight = contract_rows(normed, projected_grad)
    attn_sums = (
        lax.psum_scatter(grad_gain_one, "fsdp", scatter_dimension=0, tiled=True),
        lax.psum_scatter(grad_bias_one, "fsdp", scatter_dimension=0, tiled=True),
        lax.psum_scatter(grad_qkv_weight, "fsdp", scatter_dimension=0, tiled=True),
        lax.psum_scatter(grad_qkv_bias, "fsdp", scatter_dimension=0, tiled=True),
        lax.psum_scatter(grad_out_weight, "fsdp", scatter_dimension=0, tiled=True),
        lax.psum_scatter(grad_out_bias, "fsdp", scatter_dimension=0, tiled=True),
    )
    reduced = (
        lax.psum(attn_sums[0].astype(jnp.bfloat16), "replica").astype(jnp.float32),
        lax.psum(attn_sums[1].astype(jnp.bfloat16), "replica").astype(jnp.float32),
        lax.psum(attn_sums[2].astype(jnp.bfloat16), "replica").astype(jnp.float32),
        lax.psum(attn_sums[3].astype(jnp.bfloat16), "replica").astype(jnp.float32),
        lax.psum(attn_sums[4].astype(jnp.bfloat16), "replica").astype(jnp.float32),
        lax.psum(attn_sums[5].astype(jnp.bfloat16), "replica").astype(jnp.float32),
        lax.psum(ffn_sums[0].astype(jnp.bfloat16), "replica").astype(jnp.float32),
        lax.psum(ffn_sums[1].astype(jnp.bfloat16), "replica").astype(jnp.float32),
        lax.psum(ffn_sums[2].astype(jnp.bfloat16), "replica").astype(jnp.float32),
        lax.psum(ffn_sums[3].astype(jnp.bfloat16), "replica").astype(jnp.float32),
        lax.psum(ffn_sums[4].astype(jnp.bfloat16), "replica").astype(jnp.float32),
        lax.psum(ffn_sums[5].astype(jnp.bfloat16), "replica").astype(jnp.float32),
    )
    return (
        layer_out[None],
        input_grad[None],
        reduced[0],
        reduced[1],
        reduced[2],
        reduced[3],
        reduced[4],
        reduced[5],
        reduced[6],
        reduced[7],
        reduced[8],
        reduced[9],
        reduced[10],
        reduced[11],
    )


def solution(mesh):
    in_specs = (
        P(("fsdp", "replica"), None, None),
        P(("fsdp", "replica"), None, None),
        P(("fsdp", "replica"), None),
        P(("fsdp", "replica"), None),
        P("fsdp"),
        P("fsdp"),
        P("fsdp", None),
        P("fsdp"),
        P("fsdp", None),
        P("fsdp"),
        P("fsdp"),
        P("fsdp"),
        P("fsdp", None),
        P("fsdp"),
        P("fsdp", None),
        P("fsdp"),
    )
    out_specs = (
        P(("fsdp", "replica"), None, None),
        P(("fsdp", "replica"), None, None),
        P("fsdp"),
        P("fsdp"),
        P("fsdp", None),
        P("fsdp"),
        P("fsdp", None),
        P("fsdp"),
        P("fsdp"),
        P("fsdp"),
        P("fsdp", None),
        P("fsdp"),
        P("fsdp", None),
        P("fsdp"),
    )
    return jax.shard_map(body, mesh=mesh, in_specs=in_specs, out_specs=out_specs, check_vma=False)
```

profile of v0, /device:TPU:0, one launch (start us, length us, event | category | flops | bytes accessed | tf_op | source)
XLA Modules:
  0.0 1118.5 jit_solution(7735304638543786908)
XLA Ops:
  24.4 39.9 %all-reduce.16 = (bf16[768]{0:T(1024)(128)(2,1)}, bf16[2304]{0:T(1024)(128)(2,1)S(1)}, bf16[768]{0:T(1024)(128)(2,1)S(1)}, bf16[768]{0:T(1024)(128)(2,1)S(1)}, b...) all-reduce(bf16[768]{0:T(1024)(128)(2,1)S(1)} %dynamic-update-slice, ...), channel_id=1, replica_groups=mesh['fsdp'=8,'replica'=4] {'fsdp'}, use_global_device_ids=true, to_apply=%add.6 | all-reduce | flops 6912 | bytes 27648
  66.0 25.9 %all-gather = bf16[8,1,384]{2,1,0:T(2,128)(2,1)S(1)} all-gather(bf16[1,1,384]{2,1,0:T(2,128)(2,1)S(1)} %reshape.495), channel_id=1, replica_groups=mesh['fsdp'=8,'replica'=4] {'fsdp'}, dimensions={0}, use_global_device_ids=true | all-gather | bytes 6912 | tf_op jit(solution)/shard_map/all_gather | solution.py:218
  98.7 6.3 convolution_add_fusion
  106.3 3.0 fusion.72
  109.3 2.4 copy.88
  111.7 2.6 copy.89
  114.3 3.6 copy.85
  117.9 2.9 subtract_convert_fusion.2
  121.5 74.1 %while.27 = (s32[]{:T(128)}, bf16[2,512,12,64]{1,3,2,0:T(8,128)(2,1)}, f32[2,12,512]{2,1,0:T(8,128)S(1)}, s32[2,512]{1,0:T(2,128)S(1)}, s32[1,1024]{1,0:T(1,128)...) while((s32[]{:T(128)}, ...), condition=%wide.region_8.9_spmd, body=%wide.region_5.8_spmd.sunk | while | flops 1688727552 | bytes 190299344 | solution.py:120
  123.7 11.0 fusion.120
  134.7 12.4 %fusion.121 = f32[12,512]{1,0:T(8,128)S(1)} fusion(f32[12,512,1024]{2,1,0:T(8,128)} %get-tuple-element.584, f32[12,512]{1,0:T(8,128)S(1)} %get-tuple-element.585, pred[512,1024]{1,0:T(8,128)(4,1)S(1)} %fusion.119), kind=kLoop, calls=%fused_computation.4.clone.1 | loop fusion | flops 25159680 | bytes 25739264 | tf_op jit(solution)/shard_map/while/body/eval_jaxpr/reduce_sum | solution.py:112
  147.1 3.2 copy-done
  150.3 8.5 bitcast_dynamic-update-slice_fusion.6
  160.8 10.7 fusion.120
  171.5 12.3 %fusion.121 = f32[12,512]{1,0:T(8,128)S(1)} fusion(f32[12,512,1024]{2,1,0:T(8,128)} %get-tuple-element.584, f32[12,512]{1,0:T(8,128)S(1)} %get-tuple-element.585, pred[512,1024]{1,0:T(8,128)(4,1)S(1)} %fusion.119), kind=kLoop, calls=%fused_computation.4.clone.1 | loop fusion | flops 25159680 | bytes 25739264 | tf_op jit(solution)/shard_map/while/body/eval_jaxpr/reduce_sum | solution.py:112
  183.8 3.3 copy-done
  187.1 8.5 bitcast_dynamic-update-slice_fusion.6
  195.7 4.1 copy.90
  201.5 3.8 fusion.74
  206.1 37.9 %multiply_convert_fusion.1 = (bf16[1024,3072]{1,0:T(8,128)(2,1)}, f32[1024,3072]{1,0:T(8,128)}, f32[1024,3072]{1,0:T(8,128)}) fusion(f32[3072]{0:T(1024)S(1)} %bitcast.217, bf16[768,3072]{1,0:T(8,128)(2,1)} %all-gather.10.cloned.1.call-done, f32[1024,768]{0,1:T(8,128)S(1)} %get-tuple-element.432, f32[768]{0:T(1024)S(1)} %copy-done.60, ...), kind=kOutput, calls=%fused_computation.56 | convolution fusion | flops 5043388416 | bytes 39348224 | tf_op jit(solution)/shard_map/dot_general | solution.py:257
  244.0 37.8 %all-gather.12.cloned.1.call-done = bf16[3072,768]{1,0:T(8,128)(2,1)} async-done(((bf16[384,768]{1,0:T(8,128)(2,1)}), bf16[3072,768]{1,0:T(8,128)(2,1)}) %all-gather.12.cloned.1.call-update) | async-done | bytes 4718608 | tf_op jit(solution)/shard_map/all_gather | solution.py:219
  281.8 19.1 %convert_reduce_fusion = (f32[3072]{0:T(1024)}, bf16[1024,3072]{1,0:T(8,128)(2,1)}) fusion(f32[1024,3072]{1,0:T(8,128)} %get-tuple-element.405, bf16[3072,768]{1,0:T(8,128)(2,1)} %all-gather.12.cloned.1.call-done, bf16[1,1024,768]{2,1,0:T(8,128)(2,1)} %param.21, f32[1024,3072]{1,0:T(8,128)} %get-tuple-element.433, f32[3072]{0:T(1024)S(1)} %bitcast.218), kind=kOutput, calls=%fused_computation.54 | convolution fusion | flops 4885312512 | bytes 37773312 | tf_op jit(solution)/shard_map/dot_general | solution.py:21
  300.9 10.4 fusion.76
  311.3 3.5 copy.93
  314.8 3.5 multiply_reduce_fusion.1
  321.8 2.8 fusion.77
  324.6 2.7 convolution_convert_fusion
  331.0 233.6 %while.28 = (s32[]{:T(128)}, f32[1024,12,64]{0,2,1:T(8,128)}, f32[1024,12,64]{0,2,1:T(8,128)}, f32[2,512,12,64]{1,0,3,2:T(2,128)}, bf16[2,512,12,64]{1,3,2,0:T(8...) while((s32[]{:T(128)}, f32[1024,12,64]{0,2,1:T(8,128)}, ...), condition=%wide.region_15.16_spmd.clone, body=%wide.region_13.15_spmd.clone.sunk | while | flops 4127846400 | bytes 238230832 | solution.py:184
  333.2 11.4 %fusion.131 = f32[12,512,1024]{2,1,0:T(8,128)} fusion(bf16[1024,12,64]{0,2,1:T(8,128)(2,1)S(1)} %get-tuple-element.680, bf16[2,512,12,64]{1,3,2,0:T(8,128)(2,1)} %get-tuple-element.674, s32[]{:T(128)S(6)} %copy.152), kind=kOutput, calls=%fused_computation.35.clone.1 | convolution fusion | flops 805306368 | bytes 27525124 | tf_op jit(solution)/shard_map/while/body/eval_jaxpr/qhd,khd->hqk/dot_general | solution.py:78
  344.7 13.8 %bitcast_add_fusion.5 = f32[1024,12,64]{0,2,1:T(8,128)} fusion(f32[1024,12,64]{0,2,1:T(8,128)} %get-tuple-element.656, f32[12,512,1024]{2,1,0:T(8,128)} %fusion.131, f32[12,512]{1,0:T(8,128)S(1)} %dynamic-slice_bitcast_fusion.2, pred[512,1024]{1,0:T(8,128)(4,1)S(1)} %fusion.132, pred[]{:T(512)S(6)} %compare.3, ...), kind=kOutput, calls=%fused_computation.26.clone.1 | convolution fusion | flops 832045056 | bytes 32800772 | tf_op jit(solution)/shard_map/while/body/eval_jaxpr/hqk,qhd->khd/dot_general | solution.py:167
  358.5 18.2 %multiply_reduce_fusion.5 = (f32[12,512]{1,0:T(8,128)S(1)}, f32[12,512,1024]{2,1,0:T(8,128)}) fusion(f32[12,512,1024]{2,1,0:T(8,128)} %fusion.131, f32[12,512]{1,0:T(8,128)S(1)} %dynamic-slice_bitcast_fusion.2, pred[512,1024]{1,0:T(8,128)(4,1)S(1)} %fusion.132, bf16[1024,12,64]{0,2,1:T(8,128)(2,1)} %get-tuple-element.683, ...), kind=kOutput, calls=%fused_computation.21.clone.1 | convolution fusion | flops 836757504 | bytes 53264388 | tf_op jit(solution)/shard_map/while/body/eval_jaxpr/qhd,khd->hqk/dot_general | solution.py:151
  376.7 21.7 %multiply_convert_fusion.3 = bf16[12,512,1024]{2,1,0:T(8,128)(2,1)} fusion(f32[12,512,1024]{2,1,0:T(8,128)} %get-tuple-element.600, f32[12,512,1024]{2,1,0:T(8,128)} %fusion.131, f32[12,512]{1,0:T(8,128)S(1)} %get-tuple-element.601, f32[12,512]{1,0:T(8,128)S(1)} %dynamic-slice_bitcast_fusion.2, pred[512,1024]{1,0:T(8,128)(4,1)S(1)} %fusion.132), kind=kLoop, calls=%fused_computation.20.clone.1 | loop fusion | flops 37748736 | bytes 63488000 | tf_op jit(solution)/shard_map/while/body/eval_jaxpr/convert_element_type | solution.py:155
  398.4 9.8 multiply_bitcast_fusion.2
  408.2 8.7 bitcast_add_fusion.4
  418.6 28.8 %dynamic_update_slice.19 = f32[2,512,12,64]{1,0,3,2:T(2,128)} dynamic-update-slice(f32[2,512,12,64]{1,0,3,2:T(2,128)} %get-tuple-element.657, f32[1,512,12,64]{1,0,3,2:T(1,128)S(1)} %copy.127, s32[]{:T(128)S(6)} %copy.152, s32[]{:T(128)} %constant.33.clone.1..sunk, s32[]{:T(128)} %constant.33.clone.1..sunk, s32[]{:T(128)} %constant.33.clone.1..sunk) | dynamic-update-slice | bytes 3145732 | tf_op jit(solution)/shard_map/while/body/jit(dynamic_update_index_in_dim)/dynamic_update_slice | solution.py:120
  449.4 11.4 %fusion.131 = f32[12,512,1024]{2,1,0:T(8,128)} fusion(bf16[1024,12,64]{0,2,1:T(8,128)(2,1)S(1)} %get-tuple-element.680, bf16[2,512,12,64]{1,3,2,0:T(8,128)(2,1)} %get-tuple-element.674, s32[]{:T(128)S(6)} %copy.152), kind=kOutput, calls=%fused_computation.35.clone.1 | convolution fusion | flops 805306368 | bytes 27525124 | tf_op jit(solution)/shard_map/while/body/eval_jaxpr/qhd,khd->hqk/dot_general | solution.py:78
  460.8 14.3 %bitcast_add_fusion.5 = f32[1024,12,64]{0,2,1:T(8,128)} fusion(f32[1024,12,64]{0,2,1:T(8,128)} %get-tuple-element.656, f32[12,512,1024]{2,1,0:T(8,128)} %fusion.131, f32[12,512]{1,0:T(8,128)S(1)} %dynamic-slice_bitcast_fusion.2, pred[512,1024]{1,0:T(8,128)(4,1)S(1)} %fusion.132, pred[]{:T(512)S(6)} %compare.3, ...), kind=kOutput, calls=%fused_computation.26.clone.1 | convolution fusion | flops 832045056 | bytes 32800772 | tf_op jit(solution)/shard_map/while/body/eval_jaxpr/hqk,qhd->khd/dot_general | solution.py:167
  475.1 18.1 %multiply_reduce_fusion.5 = (f32[12,512]{1,0:T(8,128)S(1)}, f32[12,512,1024]{2,1,0:T(8,128)}) fusion(f32[12,512,1024]{2,1,0:T(8,128)} %fusion.131, f32[12,512]{1,0:T(8,128)S(1)} %dynamic-slice_bitcast_fusion.2, pred[512,1024]{1,0:T(8,128)(4,1)S(1)} %fusion.132, bf16[1024,12,64]{0,2,1:T(8,128)(2,1)} %get-tuple-element.683, ...), kind=kOutput, calls=%fused_computation.21.clone.1 | convolution fusion | flops 836757504 | bytes 53264388 | tf_op jit(solution)/shard_map/while/body/eval_jaxpr/qhd,khd->hqk/dot_general | solution.py:151
  493.2 21.2 %multiply_convert_fusion.3 = bf16[12,512,1024]{2,1,0:T(8,128)(2,1)} fusion(f32[12,512,1024]{2,1,0:T(8,128)} %get-tuple-element.600, f32[12,512,1024]{2,1,0:T(8,128)} %fusion.131, f32[12,512]{1,0:T(8,128)S(1)} %get-tuple-element.601, f32[12,512]{1,0:T(8,128)S(1)} %dynamic-slice_bitcast_fusion.2, pred[512,1024]{1,0:T(8,128)(4,1)S(1)} %fusion.132), kind=kLoop, calls=%fused_computation.20.clone.1 | loop fusion | flops 37748736 | bytes 63488000 | tf_op jit(solution)/shard_map/while/body/eval_jaxpr/convert_element_type | solution.py:155
  514.4 9.8 multiply_bitcast_fusion.2
  524.2 9.6 bitcast_add_fusion.4
  535.4 28.8 %dynamic_update_slice.19 = f32[2,512,12,64]{1,0,3,2:T(2,128)} dynamic-update-slice(f32[2,512,12,64]{1,0,3,2:T(2,128)} %get-tuple-element.657, f32[1,512,12,64]{1,0,3,2:T(1,128)S(1)} %copy.127, s32[]{:T(128)S(6)} %copy.152, s32[]{:T(128)} %constant.33.clone.1..sunk, s32[]{:T(128)} %constant.33.clone.1..sunk, s32[]{:T(128)} %constant.33.clone.1..sunk) | dynamic-update-slice | bytes 3145732 | tf_op jit(solution)/shard_map/while/body/jit(dynamic_update_index_in_dim)/dynamic_update_slice | solution.py:120
  564.6 4.3 reshape.470
  568.9 2.3 convert.46
  574.8 7.0 fusion.63
  582.5 10.5 fusion.67
  594.4 10.2 fusion.55
  607.0 8.6 fusion.75
  615.6 3.7 copy.97
  619.3 2.7 fusion.51
  624.0 9.5 fusion.58
  635.1 74.5 %reduce-scatter.5.cloned.1.call-done = f32[96,2304]{1,0:T(8,128)} async-done(((f32[768,2304]{1,0:T(8,128)}), f32[96,2304]{1,0:T(8,128)}) %reduce-scatter.5.cloned.1.call-update) | async-done | bytes 884752 | tf_op jit(solution)/shard_map/reduce_scatter | solution.py:320
  711.6 164.6 %reduce-scatter.9.cloned.1.call-done = f32[96,3072]{1,0:T(8,128)} async-done(((f32[768,3072]{1,0:T(8,128)}), f32[96,3072]{1,0:T(8,128)}) %reduce-scatter.9.cloned.1.call-update) | async-done | bytes 1179664 | tf_op jit(solution)/shard_map/reduce_scatter | solution.py:285
  876.2 2.2 convert_element_type.214
  878.3 164.5 %reduce-scatter.11.cloned.1.call-done = f32[384,768]{1,0:T(8,128)} async-done(((f32[3072,768]{1,0:T(8,128)}), f32[384,768]{1,0:T(8,128)}) %reduce-scatter.11.cloned.1.call-update) | async-done | bytes 1179664 | tf_op jit(solution)/shard_map/reduce_scatter | solution.py:287
  1042.8 2.1 convert_element_type.219
  1045.0 2.8 convert_reduce_fusion.1
  1047.8 2.6 copy.100
  1050.5 5.9 convert_reduce_fusion.2
  1056.4 35.3 %all-reduce.15 = (bf16[768]{0:T(1024)(128)(2,1)S(1)}, bf16[768]{0:T(1024)(128)(2,1)S(1)}, bf16[2304]{0:T(1024)(128)(2,1)S(1)}, bf16[768]{0:T(1024)(128)(2,1)S(1)...) all-reduce(f32[768]{0:T(1024)S(1)} %get-tuple-element.321, ...), channel_id=2, replica_groups=mesh['fsdp'=8,'replica'=4] {'fsdp'}, use_global_device_ids=true, to_apply=%region_19.20.clone | all-reduce | flops 9984 | bytes 59904
  1092.3 5.7 all-reduce.17
  1102.3 2.6 copy.101
  1106.6 2.0 convert_element_type.201
  1108.6 2.2 convert_element_type.215
  (285 shorter events, 65.7 us)
Async XLA Ops:
  7.2 91.5 %all-gather.6.cloned.1.call-start = ((), (), s32[]{:S(2)}) async-start(), calls=%async_computation.4 | async-start | bytes 3981312 | tf_op jit(solution)/shard_map/all_gather | solution.py:209
  7.9 193.5 %all-gather.8.cloned.1.call-start = ((), (), s32[]{:S(2)}) async-start(), calls=%async_computation.5 | async-start | bytes 1327104 | tf_op jit(solution)/shard_map/all_gather | solution.py:211
  8.7 197.1 %all-gather.10.cloned.1.call-start = ((), (), s32[]{:S(2)}) async-start(), calls=%async_computation.6 | async-start | bytes 5308416 | tf_op jit(solution)/shard_map/all_gather | solution.py:217
  9.4 272.4 %all-gather.12.cloned.1.call-start = ((), (), s32[]{:S(2)}) async-start(), calls=%async_computation.7 | async-start | bytes 5308416 | tf_op jit(solution)/shard_map/all_gather | solution.py:219
  10.0 623.5 %reduce-scatter.7.cloned.1.call-start = ((), (), s32[]{:S(2)}) async-start(), calls=%async_computation.9 | async-start | bytes 2654208 | tf_op jit(solution)/shard_map/reduce_scatter | solution.py:322
  64.2 34.4 %copy-start.41 = (f32[768]{0:T(1024)}, f32[768]{0:T(1024)S(1)}, u32[]{:S(2)}) copy-start(f32[768]{0:T(1024)S(1)} %convert_element_type.174) | copy-start | bytes 9220
  64.8 33.8 %copy-start.62 = (f32[768]{0:T(1024)}, f32[768]{0:T(1024)S(1)}, u32[]{:S(2)}) copy-start(f32[768]{0:T(1024)S(1)} %convert_element_type.175) | copy-start | bytes 9220
  92.6 3.2 copy-start.22
  94.4 4.2 copy-start.8
  94.7 10.3 copy-start.39
  95.8 9.2 copy-start.45
  98.6 19.3 %copy-start.25 = (f32[1024,32]{0,1:T(8,128)}, f32[1024,32]{0,1:T(8,128)S(1)}, u32[]{:S(2)}) copy-start(f32[1024,32]{0,1:T(8,128)S(1)} %get-tuple-element.428) | copy-start | bytes 393220
  123.7 23.4 %copy-start.7 = (bf16[1024,12,64]{0,2,1:T(8,128)(2,1)S(1)}, bf16[1024,12,64]{0,2,1:T(8,128)(2,1)}, u32[]{:S(2)}) copy-start(bf16[1024,12,64]{0,2,1:T(8,128)(2,1)} %get-tuple-element.636) | copy-start | bytes 4718596 | tf_op jit(solution)/shard_map/while
  134.7 15.6 %copy-start = (f32[12,512,1024]{2,1,0:T(8,128)S(1)}, f32[12,512,1024]{2,1,0:T(8,128)}, u32[]{:S(2)}) copy-start(f32[12,512,1024]{2,1,0:T(8,128)} %get-tuple-element.584) | copy-start | bytes 75497472 | tf_op jit(solution)/shard_map/while
  160.8 23.0 %copy-start.7 = (bf16[1024,12,64]{0,2,1:T(8,128)(2,1)S(1)}, bf16[1024,12,64]{0,2,1:T(8,128)(2,1)}, u32[]{:S(2)}) copy-start(bf16[1024,12,64]{0,2,1:T(8,128)(2,1)} %get-tuple-element.636) | copy-start | bytes 4718596 | tf_op jit(solution)/shard_map/while
  171.5 15.6 %copy-start = (f32[12,512,1024]{2,1,0:T(8,128)S(1)}, f32[12,512,1024]{2,1,0:T(8,128)}, u32[]{:S(2)}) copy-start(f32[12,512,1024]{2,1,0:T(8,128)} %get-tuple-element.584) | copy-start | bytes 75497472 | tf_op jit(solution)/shard_map/while
  195.6 5.8 copy-start.1
  195.6 5.8 copy-start.5
  195.6 5.8 copy-start.33
  195.6 5.8 copy-start.35
  195.7 5.8 copy-start.37
  195.7 5.8 copy-start.66
  195.7 5.8 copy-start.64
  205.3 113.1 %copy-start.12 = (f32[1024,768]{0,1:T(8,128)}, f32[1024,768]{0,1:T(8,128)S(1)}, u32[]{:S(2)}) copy-start(f32[1024,768]{0,1:T(8,128)S(1)} %get-tuple-element.432) | copy-start | bytes 9437188
  205.3 113.0 %copy-start.43 = (f32[1024]{0:T(1024)}, f32[1024]{0:T(1024)S(1)}, u32[]{:S(2)}) copy-start(f32[1024]{0:T(1024)S(1)} %broadcast_multiply_fusion) | copy-start | bytes 12292
  205.8 112.6 %copy-start.53 = (f32[1024]{0:T(1024)}, f32[1024]{0:T(1024)S(1)}, u32[]{:S(2)}) copy-start(f32[1024]{0:T(1024)S(1)} %fusion.62) | copy-start | bytes 12292
  314.8 3.6 copy-start.14
  319.3 1.7 copy-start.11
  319.3 1.7 copy-start.47
  319.8 2.0 copy-start.24
  329.3 1.6 copy-start.2
  329.3 1.6 copy-start.28
  330.9 378.7 %reduce-scatter.5.cloned.1.call-start = ((), (), s32[]{:S(2)}) async-start(), calls=%async_computation.8 | async-start | bytes 7962624 | tf_op jit(solution)/shard_map/reduce_scatter | solution.py:320
  333.2 11.4 %copy-start.15 = (bf16[2,512,12,64]{1,3,2,0:T(8,128)(2,1)S(1)}, bf16[2,512,12,64]{1,3,2,0:T(8,128)(2,1)}, u32[]{:S(2)}) copy-start(bf16[2,512,12,64]{1,3,2,0:T(8,128)(2,1)} %get-tuple-element.682) | copy-start | bytes 4718596 | tf_op jit(solution)/shard_map/while
  398.4 9.8 copy-start.6
  408.2 8.7 copy-start.4
  449.4 11.4 %copy-start.15 = (bf16[2,512,12,64]{1,3,2,0:T(8,128)(2,1)S(1)}, bf16[2,512,12,64]{1,3,2,0:T(8,128)(2,1)}, u32[]{:S(2)}) copy-start(bf16[2,512,12,64]{1,3,2,0:T(8,128)(2,1)} %get-tuple-element.682) | copy-start | bytes 4718596 | tf_op jit(solution)/shard_map/while
  514.4 9.8 copy-start.6
  524.2 9.6 copy-start.4
  568.9 2.8 copy-start.3
  568.9 2.8 copy-start.26
  568.9 2.8 copy-start.30
  571.2 1.9 copy-start.18
  572.8 2.0 copy-start.9
  572.8 2.0 copy-start.40
  572.8 2.0 copy-start.42
  572.8 2.0 copy-start.46
  572.8 2.0 copy-start.63
  573.1 1.6 copy-start.21
  581.8 294.4 %reduce-scatter.9.cloned.1.call-start = ((), (), s32[]{:S(2)}) async-start(), calls=%async_computation.10 | async-start | bytes 10616832 | tf_op jit(solution)/shard_map/reduce_scatter | solution.py:285
  593.0 449.8 %reduce-scatter.11.cloned.1.call-start = ((), (), s32[]{:S(2)}) async-start(), calls=%async_computation.11 | async-start | bytes 10616832 | tf_op jit(solution)/shard_map/reduce_scatter | solution.py:287
  604.6 2.3 copy-start.65
  604.6 2.4 copy-start.19
  604.7 500.2 %all-reduce.21.cloned.1.call-start = ((), (), s32[]{:S(2)}) async-start(), calls=%async_computation.12 | async-start | bytes 3538944 | tf_op jit(solution)/shard_map/psum | solution.py:328
  619.3 2.7 copy-start.50
  619.3 3.1 copy-start.10
  622.0 2.0 copy-start.13
  1045.0 5.4 copy-start.17
  1045.0 5.4 copy-start.48
  1050.4 5.9 copy-start.55
  1050.4 5.9 copy-start.56
  1050.4 5.9 copy-start.58
  1050.5 5.9 copy-start.59
  1104.9 5.9 copy-start.29
  (18 other events, 19.0 us)
Sparse Core Ops, SparseCore 0:
  10.2 68.4 all-gather.5
  80.9 39.8 all-gather.7
  123.0 78.6 all-gather.9
  203.8 78.0 all-gather.11
  331.0 67.1 reduce-scatter.6
  582.0 127.5 reduce-scatter.4
  713.6 162.5 reduce-scatter.8
  880.2 162.5 reduce-scatter.10
  1046.8 45.7 all-reduce.20
where the time goes:
time: 1130 us; the launch traced here: 1120 us
  waiting for transfers between devices  444 us (39%)
  matrix products  293 us (26%)
  local copies, waits for them, and re-layouts  129 us (11%)
  other arithmetic  127 us (11%)
  blocking collectives  107 us (9%)
  between operations  18.4 us (2%)
    reduce_scatter x1, waiting for transfers between devices, body(): lax.psum_scatter(grad_up_weight, 'fsdp', scatter_dimension=0, tiled=True)  165 us
    reduce_scatter x1, waiting for transfers between devices, body(): lax.psum_scatter(grad_down_weight, 'fsdp', scatter_dimension=0, tiled=True)  164 us
    unnamed x2, blocking collectives  75.2 us
    reduce_scatter x1, waiting for transfers between devices, body(): lax.psum_scatter(grad_qkv_weight, 'fsdp', scatter_dimension=0, tiled=True)  74.5 us
    dynamic_update_slice x4, local copies, waits for them, and re-layouts, attend_forward(): lax.scan(one_block, jnp.zeros((), jnp.float32), split_blocks(queries, seg...  60.9 us
    dot_general x4, matrix products, block_scores(): jnp.einsum('qhd,khd->hqk', block_queries, key_rows, preferred_element_typ...  44.4 us
    convert_element_type x2, other arithmetic, one_block(): score_grad = (weights * (weight_grad - row_dot)).astype(jnp.bfloat16)  43 us
    dot_general x4, matrix products, times_transpose(): lax.dot_general(left_matrix, right_matrix, (((1,), (1,)), ((), ())), pref...  40.8 us
  transfers between devices with their start and end apart: 9, of which 4 were waited for; matrix products, arithmetic and copies ran while one was open for 43% of the time, Pallas kernels for 0%

commit v1 on v0

--- a/solution.py
+++ b/solution.py
@@ -9,6 +9,18 @@
 GENES = 4
 EPSILON = 1e-05
 NEG_FILL = -1000000000.0
+
+
+def collect(value, axis, dim):
+    ways, here = (lax.axis_size(axis), lax.axis_index(axis))
+    grown, reach = (value, 1)
+    while reach < ways:
+        theirs = lax.ppermute(grown, axis, [(d, d ^ reach) for d in range(ways)])
+        mine_first = jnp.concatenate([grown, theirs], axis=dim)
+        theirs_first = jnp.concatenate([theirs, grown], axis=dim)
+        grown = jnp.where(here & reach == 0, mine_first, theirs_first)
+        reach = 2 * reach
+    return grown
 
 
 def contract_rows(left_matrix, right_matrix):
@@ -216,7 +228,7 @@
         lax.all_gather(ln2_bias, "fsdp", axis=0, tiled=True),
         lax.all_gather(w_up, "fsdp", axis=0, tiled=True),
         lax.all_gather(b_up, "fsdp", axis=0, tiled=True),
-        lax.all_gather(w_down, "fsdp", axis=0, tiled=True),
+        collect(w_down, "fsdp", 0),
         lax.all_gather(b_down, "fsdp", axis=0, tiled=True),
     )
     length = layer_input.shape[1]

time: 1130 us -> 1210 us (1.071)
  blocking collectives: 107 us -> 256 us
  waiting for transfers between devices: 444 us -> 369 us
    unnamed x2, blocking collectives: 75.2 us -> 223 us
    reduce_scatter x1, waiting for transfers between devices: 165 us -> 67.7 us  [body(): lax.psum_scatter(grad_up_weight, 'fsdp', scatter_dimension=0, tiled=True)]
    reduce_scatter x1, waiting for transfers between devices: 74.5 us -> 0.01 us  [body(): lax.psum_scatter(grad_qkv_weight, 'fsdp', scatter_dimension=0, tiled=True)]
    ppermute x0 -> x3, waiting for transfers between devices: none -> 61 us  [collect(): theirs = lax.ppermute(grown, axis, [(d, d ^ reach) for d in range(ways)])]
    psum x1, waiting for transfers between devices: 0.01 us -> 34.3 us  [body(): lax.psum(attn_sums[2].astype(jnp.bfloat16), 'replica').astype(jnp.float32)]
    unnamed x158 -> x174, local copies, waits for them, and re-layouts: 28.4 us -> 29 us
  transfers between devices with their start and end apart: 9 -> 12, of which waited for: 4 -> 6; matrix products, arithmetic and copies ran while one was open for 43% -> 41% of each run, Pallas kernels for 0% -> 0%
where the time goes in v1:
time: 1210 us; the launch traced here: 1200 us
  waiting for transfers between devices  369 us (30%)
  matrix products  294 us (24%)
  blocking collectives  256 us (21%)
  local copies, waits for them, and re-layouts  133 us (11%)
  other arithmetic  127 us (10%)
  between operations  18.3 us (2%)
    unnamed x2, blocking collectives  223 us
    reduce_scatter x1, waiting for transfers between devices, body(): lax.psum_scatter(grad_down_weight, 'fsdp', scatter_dimension=0, tiled=True)  164 us
    reduce_scatter x1, waiting for transfers between devices, body(): lax.psum_scatter(grad_up_weight, 'fsdp', scatter_dimension=0, tiled=True)  67.7 us
    dynamic_update_slice x4, local copies, waits for them, and re-layouts, attend_forward(): lax.scan(one_block, jnp.zeros((), jnp.float32), split_blocks(queries, seg...  63.4 us
    ppermute x3, waiting for transfers between devices, collect(): theirs = lax.ppermute(grown, axis, [(d, d ^ reach) for d in range(ways)])  61 us
    dot_general x4, matrix products, block_scores(): jnp.einsum('qhd,khd->hqk', block_queries, key_rows, preferred_element_typ...  45.1 us
    convert_element_type x2, other arithmetic, one_block(): score_grad = (weights * (weight_grad - row_dot)).astype(jnp.bfloat16)  43.4 us
    dot_general x4, matrix products, times_transpose(): lax.dot_general(left_matrix, right_matrix, (((1,), (1,)), ((), ())), pref...  39.9 us
  transfers between devices with their start and end apart: 12, of which 6 were waited for; matrix products, arithmetic and copies ran while one was open for 41% of the time, Pallas kernels for 0%

profile of v1, /device:TPU:0, one launch (start us, length us, event | category | flops | bytes accessed | tf_op | source)
XLA Modules:
  0.0 1201.0 jit_solution(4327194773669691300)
XLA Ops:
  18.7 39.6 %all-reduce.16 = (bf16[768]{0:T(1024)(128)(2,1)}, bf16[2304]{0:T(1024)(128)(2,1)S(1)}, bf16[768]{0:T(1024)(128)(2,1)S(1)}, bf16[768]{0:T(1024)(128)(2,1)S(1)}, b...) all-reduce(bf16[768]{0:T(1024)(128)(2,1)S(1)} %dynamic-update-slice, ...), channel_id=1, replica_groups=mesh['fsdp'=8,'replica'=4] {'fsdp'}, use_global_device_ids=true, to_apply=%add.6 | all-reduce | flops 6912 | bytes 27648
  65.0 26.5 %all-gather = bf16[8,1,384]{2,1,0:T(2,128)(2,1)S(1)} all-gather(bf16[1,1,384]{2,1,0:T(2,128)(2,1)S(1)} %reshape.495), channel_id=1, replica_groups=mesh['fsdp'=8,'replica'=4] {'fsdp'}, dimensions={0}, use_global_device_ids=true | all-gather | bytes 6912 | tf_op jit(solution)/shard_map/all_gather | solution.py:230
  95.0 6.3 convolution_add_fusion
  101.4 3.1 fusion.80
  105.8 2.4 copy.85
  108.2 3.6 copy.88
  111.8 4.3 subtract_convert_fusion.2
  116.2 2.6 copy.89
  120.6 74.0 %while.27 = (s32[]{:T(128)}, bf16[2,512,12,64]{1,3,2,0:T(8,128)(2,1)}, f32[2,12,512]{2,1,0:T(8,128)S(1)}, s32[2,512]{1,0:T(2,128)S(1)}, s32[1,1024]{1,0:T(1,128)...) while((s32[]{:T(128)}, ...), condition=%wide.region_8.9_spmd, body=%wide.region_5.8_spmd.sunk | while | flops 1688727552 | bytes 190299856 | solution.py:132
  122.8 11.0 fusion.127
  133.8 12.4 %fusion.128 = f32[12,512]{1,0:T(8,128)S(1)} fusion(f32[12,512,1024]{2,1,0:T(8,128)} %get-tuple-element.584, f32[12,512]{1,0:T(8,128)S(1)} %get-tuple-element.585, pred[512,1024]{1,0:T(8,128)(4,1)S(1)} %fusion.126), kind=kLoop, calls=%fused_computation.4.clone.1 | loop fusion | flops 25159680 | bytes 25739264 | tf_op jit(solution)/shard_map/while/body/eval_jaxpr/reduce_sum | solution.py:124
  146.2 3.2 copy-done
  149.4 8.5 bitcast_dynamic-update-slice_fusion.6
  159.9 10.7 fusion.127
  170.6 12.4 %fusion.128 = f32[12,512]{1,0:T(8,128)S(1)} fusion(f32[12,512,1024]{2,1,0:T(8,128)} %get-tuple-element.584, f32[12,512]{1,0:T(8,128)S(1)} %get-tuple-element.585, pred[512,1024]{1,0:T(8,128)(4,1)S(1)} %fusion.126), kind=kLoop, calls=%fused_computation.4.clone.1 | loop fusion | flops 25159680 | bytes 25739264 | tf_op jit(solution)/shard_map/while/body/eval_jaxpr/reduce_sum | solution.py:124
  183.0 3.1 copy-done
  186.1 8.5 bitcast_dynamic-update-slice_fusion.6
  194.6 4.2 copy.90
  200.4 3.8 fusion.82
  205.0 37.8 %multiply_convert_fusion.1 = (bf16[1024,3072]{1,0:T(8,128)(2,1)}, f32[1024,3072]{1,0:T(8,128)}, f32[1024,3072]{1,0:T(8,128)}) fusion(f32[3072]{0:T(1024)S(1)} %bitcast.216, bf16[768,3072]{1,0:T(8,128)(2,1)} %all-gather.10.cloned.1.call-done, f32[1024,768]{0,1:T(8,128)S(1)} %get-tuple-element.432, f32[768]{0:T(1024)S(1)} %copy-done.69, ...), kind=kOutput, calls=%fused_computation.56 | convolution fusion | flops 5043388416 | bytes 39348224 | tf_op jit(solution)/shard_map/dot_general | solution.py:269
  242.9 38.8 %all-gather.12.cloned.1.call-done = bf16[3072,768]{1,0:T(8,128)(2,1)} async-done(((bf16[384,768]{1,0:T(8,128)(2,1)}), bf16[3072,768]{1,0:T(8,128)(2,1)}) %all-gather.12.cloned.1.call-update) | async-done | bytes 4718608 | tf_op jit(solution)/shard_map/all_gather | solution.py:281
  281.7 19.2 %convert_reduce_fusion = (f32[3072]{0:T(1024)}, bf16[1024,3072]{1,0:T(8,128)(2,1)}) fusion(f32[1024,3072]{1,0:T(8,128)} %get-tuple-element.405, bf16[3072,768]{1,0:T(8,128)(2,1)} %all-gather.12.cloned.1.call-done, bf16[1,1024,768]{2,1,0:T(8,128)(2,1)} %param.21, f32[1024,3072]{1,0:T(8,128)} %get-tuple-element.433, f32[3072]{0:T(1024)S(1)} %bitcast.217), kind=kOutput, calls=%fused_computation.54 | convolution fusion | flops 4885312512 | bytes 37773312 | tf_op jit(solution)/shard_map/dot_general | solution.py:33
  300.9 10.4 fusion.84
  311.3 3.5 copy.93
  314.8 3.5 multiply_reduce_fusion.1
  321.8 3.0 fusion.85
  324.9 2.7 convolution_convert_fusion
  330.8 2.9 copy.95
  333.8 237.0 %while.28 = (s32[]{:T(128)}, f32[1024,12,64]{0,2,1:T(8,128)}, f32[1024,12,64]{0,2,1:T(8,128)}, f32[2,512,12,64]{1,0,3,2:T(2,128)}, bf16[2,512,12,64]{1,3,2,0:T(8...) while((s32[]{:T(128)}, f32[1024,12,64]{0,2,1:T(8,128)}, ...), condition=%wide.region_15.16_spmd.clone, body=%wide.region_13.15_spmd.clone.sunk | while | flops 4127846400 | bytes 229843728 | solution.py:196
  336.0 11.8 fusion.138
  347.9 18.2 %multiply_reduce_fusion.5 = (f32[12,512]{1,0:T(8,128)S(1)}, f32[12,512,1024]{2,1,0:T(8,128)}) fusion(f32[12,512,1024]{2,1,0:T(8,128)} %fusion.138, f32[12,512]{1,0:T(8,128)S(1)} %dynamic-slice_bitcast_fusion.2, pred[512,1024]{1,0:T(8,128)(4,1)S(1)} %fusion.139, bf16[1024,12,64]{0,2,1:T(8,128)(2,1)} %get-tuple-element.683, ...), kind=kOutput, calls=%fused_computation.21.clone.1 | convolution fusion | flops 836757504 | bytes 53264896 | tf_op jit(solution)/shard_map/while/body/eval_jaxpr/qhd,khd->hqk/dot_general | solution.py:163
  366.1 22.1 %multiply_convert_fusion.3 = bf16[12,512,1024]{2,1,0:T(8,128)(2,1)} fusion(f32[12,512,1024]{2,1,0:T(8,128)} %get-tuple-element.600, f32[12,512,1024]{2,1,0:T(8,128)} %fusion.138, f32[12,512]{1,0:T(8,128)S(1)} %get-tuple-element.601, f32[12,512]{1,0:T(8,128)S(1)} %dynamic-slice_bitcast_fusion.2, pred[512,1024]{1,0:T(8,128)(4,1)S(1)} %fusion.139), kind=kLoop, calls=%fused_computation.20.clone.1 | loop fusion | flops 37748736 | bytes 63488000 | tf_op jit(solution)/shard_map/while/body/eval_jaxpr/convert_element_type | solution.py:167
  388.2 9.7 multiply_bitcast_fusion.2
  397.9 3.0 copy.127
  400.9 28.7 %dynamic_update_slice.19 = f32[2,512,12,64]{1,0,3,2:T(2,128)} dynamic-update-slice(f32[2,512,12,64]{1,0,3,2:T(2,128)} %get-tuple-element.657, f32[1,512,12,64]{1,0,3,2:T(1,128)S(1)} %copy.127, s32[]{:T(128)} %get-tuple-element.654, s32[]{:T(128)} %constant.35.clone.1..sunk, s32[]{:T(128)} %constant.35.clone.1..sunk, s32[]{:T(128)} %constant.35.clone.1..sunk) | dynamic-update-slice | bytes 3145732 | tf_op jit(solution)/shard_map/while/body/jit(dynamic_update_index_in_dim)/dynamic_update_slice | solution.py:132
  429.6 8.9 bitcast_add_fusion.4
  438.5 13.4 %bitcast_add_fusion.5 = f32[1024,12,64]{0,2,1:T(8,128)} fusion(f32[1024,12,64]{0,2,1:T(8,128)} %get-tuple-element.656, f32[12,512,1024]{2,1,0:T(8,128)} %fusion.138, f32[12,512]{1,0:T(8,128)S(1)} %dynamic-slice_bitcast_fusion.2, pred[512,1024]{1,0:T(8,128)(4,1)S(1)} %copy-done.5, pred[]{:T(512)S(6)} %compare.3, ...), kind=kOutput, calls=%fused_computation.26.clone.1 | convolution fusion | flops 832045056 | bytes 32800772 | tf_op jit(solution)/shard_map/while/body/eval_jaxpr/hqk,qhd->khd/dot_general | solution.py:179
  454.0 11.5 fusion.138
  465.5 18.1 %multiply_reduce_fusion.5 = (f32[12,512]{1,0:T(8,128)S(1)}, f32[12,512,1024]{2,1,0:T(8,128)}) fusion(f32[12,512,1024]{2,1,0:T(8,128)} %fusion.138, f32[12,512]{1,0:T(8,128)S(1)} %dynamic-slice_bitcast_fusion.2, pred[512,1024]{1,0:T(8,128)(4,1)S(1)} %fusion.139, bf16[1024,12,64]{0,2,1:T(8,128)(2,1)} %get-tuple-element.683, ...), kind=kOutput, calls=%fused_computation.21.clone.1 | convolution fusion | flops 836757504 | bytes 53264896 | tf_op jit(solution)/shard_map/while/body/eval_jaxpr/qhd,khd->hqk/dot_general | solution.py:163
  483.6 21.2 %multiply_convert_fusion.3 = bf16[12,512,1024]{2,1,0:T(8,128)(2,1)} fusion(f32[12,512,1024]{2,1,0:T(8,128)} %get-tuple-element.600, f32[12,512,1024]{2,1,0:T(8,128)} %fusion.138, f32[12,512]{1,0:T(8,128)S(1)} %get-tuple-element.601, f32[12,512]{1,0:T(8,128)S(1)} %dynamic-slice_bitcast_fusion.2, pred[512,1024]{1,0:T(8,128)(4,1)S(1)} %fusion.139), kind=kLoop, calls=%fused_computation.20.clone.1 | loop fusion | flops 37748736 | bytes 63488000 | tf_op jit(solution)/shard_map/while/body/eval_jaxpr/convert_element_type | solution.py:167
  504.9 9.6 multiply_bitcast_fusion.2
  514.5 3.0 copy.127
  517.6 28.7 %dynamic_update_slice.19 = f32[2,512,12,64]{1,0,3,2:T(2,128)} dynamic-update-slice(f32[2,512,12,64]{1,0,3,2:T(2,128)} %get-tuple-element.657, f32[1,512,12,64]{1,0,3,2:T(1,128)S(1)} %copy.127, s32[]{:T(128)} %get-tuple-element.654, s32[]{:T(128)} %constant.35.clone.1..sunk, s32[]{:T(128)} %constant.35.clone.1..sunk, s32[]{:T(128)} %constant.35.clone.1..sunk) | dynamic-update-slice | bytes 3145732 | tf_op jit(solution)/shard_map/while/body/jit(dynamic_update_index_in_dim)/dynamic_update_slice | solution.py:132
  546.2 9.8 bitcast_add_fusion.4
  556.1 14.3 %bitcast_add_fusion.5 = f32[1024,12,64]{0,2,1:T(8,128)} fusion(f32[1024,12,64]{0,2,1:T(8,128)} %get-tuple-element.656, f32[12,512,1024]{2,1,0:T(8,128)} %fusion.138, f32[12,512]{1,0:T(8,128)S(1)} %dynamic-slice_bitcast_fusion.2, pred[512,1024]{1,0:T(8,128)(4,1)S(1)} %copy-done.5, pred[]{:T(512)S(6)} %compare.3, ...), kind=kOutput, calls=%fused_computation.26.clone.1 | convolution fusion | flops 832045056 | bytes 32800772 | tf_op jit(solution)/shard_map/while/body/eval_jaxpr/hqk,qhd->khd/dot_general | solution.py:179
  570.7 4.3 reshape.470
  580.9 7.0 fusion.71
  588.6 10.5 fusion.75
  600.6 10.2 fusion.62
  611.6 20.3 %collective-permute-done = bf16[384,768]{1,0:T(8,128)(2,1)} collective-permute-done((bf16[384,768]{1,0:T(8,128)(2,1)}, bf16[384,768]{1,0:T(8,128)(2,1)}, u32[]{:S(2)}, u32[]{:S(2)}) %collective-permute-start) | collective-permute-done | bytes 589856 | tf_op jit(solution)/shard_map/ppermute | solution.py:18
  631.9 3.0 maximum_select_fusion.7
  637.1 40.7 %collective-permute-done.1 = bf16[768,768]{1,0:T(8,128)(2,1)} collective-permute-done((bf16[768,768]{1,0:T(8,128)(2,1)}, bf16[768,768]{1,0:T(8,128)(2,1)}, u32[]{:S(2)}, u32[]{:S(2)}) %collective-permute-start.1) | collective-permute-done | bytes 1179680 | tf_op jit(solution)/shard_map/ppermute | solution.py:18
  677.8 4.0 maximum_select_fusion.2
  681.8 2.4 collective-permute-start.2
  684.2 7.6 fusion.83
  691.8 3.6 copy.97
  695.4 2.6 fusion.58
  704.5 183.7 %all-reduce.15 = (bf16[768]{0:T(1024)(128)(2,1)S(1)}, bf16[768]{0:T(1024)(128)(2,1)S(1)}, bf16[2304]{0:T(1024)(128)(2,1)S(1)}, bf16[768]{0:T(1024)(128)(2,1)S(1)...) all-reduce(f32[768]{0:T(1024)S(1)} %get-tuple-element.321, ...), channel_id=2, replica_groups=mesh['fsdp'=8,'replica'=4] {'fsdp'}, use_global_device_ids=true, to_apply=%region_19.20.clone | all-reduce | flops 9984 | bytes 59904
  888.8 5.9 all-reduce.17
  904.3 67.7 %reduce-scatter.9.cloned.1.call-done = f32[96,3072]{1,0:T(8,128)} async-done(((f32[768,3072]{1,0:T(8,128)}), f32[96,3072]{1,0:T(8,128)}) %reduce-scatter.9.cloned.1.call-update) | async-done | bytes 1179664 | tf_op jit(solution)/shard_map/reduce_scatter | solution.py:297
  974.2 164.3 %reduce-scatter.11.cloned.1.call-done = f32[384,768]{1,0:T(8,128)} async-done(((f32[3072,768]{1,0:T(8,128)}), f32[384,768]{1,0:T(8,128)}) %reduce-scatter.11.cloned.1.call-update) | async-done | bytes 1179664 | tf_op jit(solution)/shard_map/reduce_scatter | solution.py:299
  1140.7 10.6 fusion.65
  1151.3 2.6 copy.100
  1153.9 34.3 %all-reduce.21.cloned.1.call-done = (bf16[96,2304]{1,0:T(8,128)(2,1)}, bf16[96,768]{1,0:T(8,128)(2,1)}, bf16[96,3072]{1,0:T(8,128)(2,1)}, bf16[384,768]{1,0:T(8,128)(2,1)}) async-done(((bf16[96,2304]{1,0:T(8,128)(2,1)}, bf16[96,768]{1,0:T(8,128)(2,1)}, bf16[96,3072]{1,0:T(8,128)(2,1)}, bf16[384,768]{1,0:T(8,128)(2,1)}), (bf16[96,2304]{1,0:T(8,128)(2,1)}, bf16[96,768]{1,0:T(8,128)(2,1)}, ...) | async-done | bytes 1769488 | tf_op jit(solution)/shard_map/psum | solution.py:340
  (309 shorter events, 76.0 us)
Async XLA Ops:
  7.2 87.8 %all-gather.6.cloned.1.call-start = ((), (), s32[]{:S(2)}) async-start(), calls=%async_computation.4 | async-start | bytes 3981312 | tf_op jit(solution)/shard_map/all_gather | solution.py:221
  7.9 192.5 %all-gather.8.cloned.1.call-start = ((), (), s32[]{:S(2)}) async-start(), calls=%async_computation.5 | async-start | bytes 1327104 | tf_op jit(solution)/shard_map/all_gather | solution.py:223
  8.7 196.1 %all-gather.10.cloned.1.call-start = ((), (), s32[]{:S(2)}) async-start(), calls=%async_computation.6 | async-start | bytes 5308416 | tf_op jit(solution)/shard_map/all_gather | solution.py:229
  9.4 272.3 %all-gather.12.cloned.1.call-start = ((), (), s32[]{:S(2)}) async-start(), calls=%async_computation.7 | async-start | bytes 5308416 | tf_op jit(solution)/shard_map/all_gather | solution.py:281
  10.0 890.6 %reduce-scatter.7.cloned.1.call-start = ((), (), s32[]{:S(2)}) async-start(), calls=%async_computation.9 | async-start | bytes 2654208 | tf_op jit(solution)/shard_map/reduce_scatter | solution.py:334
  58.2 36.8 %copy-start.48 = (f32[768]{0:T(1024)}, f32[768]{0:T(1024)S(1)}, u32[]{:S(2)}) copy-start(f32[768]{0:T(1024)S(1)} %convert_element_type.174) | copy-start | bytes 9220
  58.2 36.8 %copy-start.67 = (f32[768]{0:T(1024)}, f32[768]{0:T(1024)S(1)}, u32[]{:S(2)}) copy-start(f32[768]{0:T(1024)S(1)} %convert_element_type.175) | copy-start | bytes 9220
  58.3 2.7 copy-start.33
  58.3 4.3 copy-start.36
  58.3 6.7 copy-start.73
  58.3 33.8 %copy-start.28 = (bf16[1,1024,768]{2,1,0:T(8,128)(2,1)S(1)}, bf16[1,1024,768]{2,1,0:T(8,128)(2,1)}, u32[]{:S(2)}) copy-start(bf16[1,1024,768]{2,1,0:T(8,128)(2,1)} %param.21) | copy-start | bytes 4718596
  60.1 34.9 %copy-start.8 = (bf16[1,1024,768]{1,2,0:T(8,128)(2,1)}, bf16[1,1024,768]{1,2,0:T(8,128)(2,1)S(1)}, u32[]{:S(2)}) copy-start(bf16[1,1024,768]{1,2,0:T(8,128)(2,1)S(1)} %copy.84) | copy-start | bytes 4718596
  60.4 40.9 %copy-start.46 = (f32[1024]{0:T(1024)}, f32[1024]{0:T(1024)S(1)}, u32[]{:S(2)}) copy-start(f32[1024]{0:T(1024)S(1)} %broadcast_multiply_fusion.1) | copy-start | bytes 12292
  60.9 40.5 %copy-start.52 = (f32[1024]{0:T(1024)}, f32[1024]{0:T(1024)S(1)}, u32[]{:S(2)}) copy-start(f32[1024]{0:T(1024)S(1)} %fusion.68) | copy-start | bytes 12292
  95.0 16.8 %copy-start.31 = (f32[1024,32]{0,1:T(8,128)}, f32[1024,32]{0,1:T(8,128)S(1)}, u32[]{:S(2)}) copy-start(f32[1024,32]{0,1:T(8,128)S(1)} %get-tuple-element.428) | copy-start | bytes 393220
  122.8 23.4 %copy-start.7 = (bf16[1024,12,64]{0,2,1:T(8,128)(2,1)S(1)}, bf16[1024,12,64]{0,2,1:T(8,128)(2,1)}, u32[]{:S(2)}) copy-start(bf16[1024,12,64]{0,2,1:T(8,128)(2,1)} %get-tuple-element.636) | copy-start | bytes 4718596 | tf_op jit(solution)/shard_map/while
  133.8 15.6 %copy-start = (f32[12,512,1024]{2,1,0:T(8,128)S(1)}, f32[12,512,1024]{2,1,0:T(8,128)}, u32[]{:S(2)}) copy-start(f32[12,512,1024]{2,1,0:T(8,128)} %get-tuple-element.584) | copy-start | bytes 75497472 | tf_op jit(solution)/shard_map/while
  159.9 23.1 %copy-start.7 = (bf16[1024,12,64]{0,2,1:T(8,128)(2,1)S(1)}, bf16[1024,12,64]{0,2,1:T(8,128)(2,1)}, u32[]{:S(2)}) copy-start(bf16[1024,12,64]{0,2,1:T(8,128)(2,1)} %get-tuple-element.636) | copy-start | bytes 4718596 | tf_op jit(solution)/shard_map/while
  170.6 15.5 %copy-start = (f32[12,512,1024]{2,1,0:T(8,128)S(1)}, f32[12,512,1024]{2,1,0:T(8,128)}, u32[]{:S(2)}) copy-start(f32[12,512,1024]{2,1,0:T(8,128)} %get-tuple-element.584) | copy-start | bytes 75497472 | tf_op jit(solution)/shard_map/while
  194.6 5.8 copy-start.1
  194.6 5.8 copy-start.6
  194.6 5.8 copy-start.39
  194.6 5.8 copy-start.42
  194.6 5.8 copy-start.44
  194.6 5.8 copy-start.74
  194.6 5.8 copy-start.71
  204.3 114.1 %copy-start.11 = (f32[1024,768]{0,1:T(8,128)}, f32[1024,768]{0,1:T(8,128)S(1)}, u32[]{:S(2)}) copy-start(f32[1024,768]{0,1:T(8,128)S(1)} %get-tuple-element.432) | copy-start | bytes 9437188
  204.3 114.0 %copy-start.50 = (f32[1024]{0:T(1024)}, f32[1024]{0:T(1024)S(1)}, u32[]{:S(2)}) copy-start(f32[1024]{0:T(1024)S(1)} %broadcast_multiply_fusion) | copy-start | bytes 12292
  204.7 113.7 %copy-start.60 = (f32[1024]{0:T(1024)}, f32[1024]{0:T(1024)S(1)}, u32[]{:S(2)}) copy-start(f32[1024]{0:T(1024)S(1)} %fusion.69) | copy-start | bytes 12292
  314.8 3.6 copy-start.15
  324.8 577.3 %reduce-scatter.5.cloned.1.call-start = ((), (), s32[]{:S(2)}) async-start(), calls=%async_computation.8 | async-start | bytes 7962624 | tf_op jit(solution)/shard_map/reduce_scatter | solution.py:332
  328.4 5.3 copy-start.2
  328.4 5.3 copy-start.34
  328.4 5.3 copy-start.37
  328.4 5.3 copy-start.40
  328.4 5.3 copy-start.43
  328.4 5.3 copy-start.45
  328.4 5.3 copy-start.75
  336.0 30.1 %copy-start.4 = (pred[512,1024]{1,0:T(8,128)(4,1)}, pred[512,1024]{1,0:T(8,128)(4,1)S(1)}, u32[]{:S(2)}) copy-start(pred[512,1024]{1,0:T(8,128)(4,1)S(1)} %fusion.139) | copy-start | bytes 1572868 | tf_op jit(solution)/shard_map/while
  429.6 9.0 copy-start.5
  429.6 9.0 copy-start.16
  454.0 29.7 %copy-start.4 = (pred[512,1024]{1,0:T(8,128)(4,1)}, pred[512,1024]{1,0:T(8,128)(4,1)S(1)}, u32[]{:S(2)}) copy-start(pred[512,1024]{1,0:T(8,128)(4,1)S(1)} %fusion.139) | copy-start | bytes 1572868 | tf_op jit(solution)/shard_map/while
  546.2 9.8 copy-start.5
  546.2 9.8 copy-start.16
  575.0 2.8 copy-start.3
  575.0 2.8 copy-start.32
  575.0 2.8 copy-start.35
  588.0 384.0 %reduce-scatter.9.cloned.1.call-start = ((), (), s32[]{:S(2)}) async-start(), calls=%async_computation.10 | async-start | bytes 10616832 | tf_op jit(solution)/shard_map/reduce_scatter | solution.py:297
  599.2 539.3 %reduce-scatter.11.cloned.1.call-start = ((), (), s32[]{:S(2)}) async-start(), calls=%async_computation.11 | async-start | bytes 10616832 | tf_op jit(solution)/shard_map/reduce_scatter | solution.py:299
  610.8 26.2 %copy-start.72 = (bf16[768]{0:T(1024)(128)(2,1)S(1)}, bf16[768]{0:T(1024)(128)(2,1)}, u32[]{:S(2)}) copy-start(bf16[768]{0:T(1024)(128)(2,1)} %get-tuple-element.381) | copy-start | bytes 4612
  610.8 577.4 %all-reduce.21.cloned.1.call-start = ((), (), s32[]{:S(2)}) async-start(), calls=%async_computation.12 | async-start | bytes 3538944 | tf_op jit(solution)/shard_map/psum | solution.py:340
  610.9 21.0 %collective-permute-start = (bf16[384,768]{1,0:T(8,128)(2,1)}, bf16[384,768]{1,0:T(8,128)(2,1)}, u32[]{:S(2)}, u32[]{:S(2)}) collective-permute-start(bf16[384,768]{1,0:T(8,128)(2,1)} %param.34), channel_id=1, source_target_pairs={{0,4},{4,0},{8,12},{12,8},{16,20},{20,16},{24,28},{28,24},{1,5},{5... | collective-permute-start | bytes 1769480 | tf_op jit(solution)/shard_map/ppermute | solution.py:18
  611.6 72.6 %copy-start.20 = (bf16[1024,12,64]{0,2,1:T(8,128)(2,1)S(1)}, bf16[1024,12,64]{0,2,1:T(8,128)(2,1)}, u32[]{:S(2)}) copy-start(bf16[1024,12,64]{0,2,1:T(8,128)(2,1)} %copy-done.19) | copy-start | bytes 4718596
  634.9 42.9 %collective-permute-start.1 = (bf16[768,768]{1,0:T(8,128)(2,1)}, bf16[768,768]{1,0:T(8,128)(2,1)}, u32[]{:S(2)}, u32[]{:S(2)}) collective-permute-start(bf16[768,768]{1,0:T(8,128)(2,1)} %maximum_select_fusion.7), channel_id=1, source_target_pairs={{0,8},{4,12},{8,0},{12,4},{16,24},{20,28},{24,16},{28,20},{1,9},{5... | collective-permute-start | bytes 3538952 | tf_op jit(solution)/shard_map/ppermute | solution.py:18
  637.0 47.1 %copy-start.22 = (bf16[1024,12,64]{0,2,1:T(8,128)(2,1)S(1)}, bf16[1024,12,64]{0,2,1:T(8,128)(2,1)}, u32[]{:S(2)}) copy-start(bf16[1024,12,64]{0,2,1:T(8,128)(2,1)} %copy-done.21) | copy-start | bytes 4718596
  637.0 47.1 %copy-start.25 = (bf16[1024,12,64]{0,2,1:T(8,128)(2,1)S(1)}, bf16[1024,12,64]{0,2,1:T(8,128)(2,1)}, u32[]{:S(2)}) copy-start(bf16[1024,12,64]{0,2,1:T(8,128)(2,1)} %copy-done.24) | copy-start | bytes 4718596
  681.8 458.9 %collective-permute-start.2 = (bf16[1536,768]{1,0:T(8,128)(2,1)}, bf16[1536,768]{1,0:T(8,128)(2,1)}, u32[]{:S(2)}, u32[]{:S(2)}) collective-permute-start(bf16[1536,768]{1,0:T(8,128)(2,1)} %maximum_select_fusion.2), channel_id=1, source_target_pairs={{0,16},{4,20},{8,24},{12,28},{16,0},{20,4},{24,8},{28,12},{1,17},{... | collective-permute-start | bytes 7077896 | tf_op jit(solution)/shard_map/ppermute | solution.py:18
  695.4 2.8 copy-start.10
  699.6 2.6 copy-start.14
  699.6 3.1 copy-start.18
  699.6 3.1 copy-start.55
  902.2 238.5 %copy-start.12 = (f32[1024,768]{0,1:T(8,128)S(1)}, f32[1024,768]{0,1:T(8,128)}, u32[]{:S(2)}) copy-start(f32[1024,768]{0,1:T(8,128)} %copy-done.11) | copy-start | bytes 9437188
  1188.2 4.4 copy-start.38
  1188.2 5.4 copy-start.41
  (29 other events, 43.7 us)
Sparse Core Ops, SparseCore 0:
  10.2 68.5 all-gather.5
  80.9 39.6 all-gather.7
  122.8 78.7 all-gather.9
  203.7 78.0 all-gather.11
  325.0 67.3 reduce-scatter.6
  588.1 191.3 reduce-scatter.4
  783.5 188.4 reduce-scatter.8
  976.0 162.3 reduce-scatter.10
  1142.4 45.6 all-reduce.20
